TPU v7x, 32 devices: a whole 2x2x4 slice. The times are simulated.
32 devices in a mesh: row: 4 (over y, x), col: 8 (over z, core).
Axes of the slice: x: 2, y: 2, z: 4, core: 2. Of those that a mesh axis runs over, the one named last changes fastest.
Arguments:
- pair_rep: float32 [64, 64, 128], P('row', 'col'), may hold values from -160 to 160
- ln_gain: float32 [128], replicated, may hold values from 0.25 to 1.75
- ln_bias: float32 [128], replicated, may hold values from -3 to 3
- w_in: float32 [1024, 128], replicated, may hold values from -0.5 to 0.5
- w_out: float32 [512, 128], replicated, may hold values from -0.25 to 0.25
- w_pde: float32 [128, 64], replicated, may hold values from -2 to 2
- labels: int32 [64, 64], P('row', 'col'), may hold values from 0 to 63
- pair_mask: int32 [64, 64], P('row', 'col'), may hold values from 0 to 1, as said below
Outputs:
- mean_loss: float32 [], replicated
- d_pair_rep: float32 [64, 64, 128], P('row', 'col')
- d_ln_gain: float32 [128], replicated
- d_ln_bias: float32 [128], replicated
- d_w_in: float32 [1024, 128], P(('row', 'col'))
- d_w_out: float32 [512, 128], P(('row', 'col'))
- d_w_pde: float32 [128, 64], replicated
Inputs may be any that keep to these rules, and one draw needn't show every extreme that they name: pair_mask[i][j] = m_i m_j for a flag m_i of token i, with m_i = 1 whenever i is a multiple of 16.
All inputs are finite; a program needn't handle non-finite values.
Results may differ from a plain program's by a relative error of at most 0.0003.
Values sent between devices are 32-bit elements; how exact they have to be, the bound alone decides.
A program may use at most 64 MiB of HBM per device.

v0:
```python
import jax
import jax.numpy as jnp
from jax import lax
from jax.sharding import PartitionSpec as P

epsilon = 1e-05


def transition(rows_block, ln_gain, ln_bias, w_in, w_out):
    average = jnp.mean(rows_block, axis=-1, keepdims=True)
    centred = rows_block - average
    variance = jnp.mean(centred * centred, axis=-1, keepdims=True)
    normed = centred * lax.rsqrt(variance + epsilon) * ln_gain + ln_bias
    projected_in = lax.dot_general(
        normed,
        w_in,
        (((1,), (1,)), ((), ())),
        precision=lax.Precision.HIGHEST,
        preferred_element_type=jnp.float32,
    )
    hidden_units = w_out.shape[0]
    hidden = jax.nn.silu(projected_in[:, :hidden_units]) * projected_in[:, hidden_units:]
    return rows_block + jnp.dot(
        hidden, w_out, precision=lax.Precision.HIGHEST, preferred_element_type=jnp.float32
    )


def group_rows(tile_rows, tile_cols):
    stride_rows = 1
    while (
        stride_rows < tile_rows
        and stride_rows * tile_cols < 1024
        and (tile_rows % (stride_rows * 2) == 0)
    ):
        stride_rows = stride_rows * 2
    return stride_rows


def mirror(tile):
    row_devices = lax.axis_size("row")
    col_devices = lax.axis_size("col")
    factor = col_devices // row_devices
    tile_cols = tile.shape[1]
    channels = tile.shape[2]
    slab_rows = tile_cols // row_devices
    pieces = tile.reshape(factor, row_devices, slab_rows, tile_cols * channels)
    pieces = lax.all_to_all(
        lax.all_to_all(pieces, "row", split_axis=1, concat_axis=0, tiled=True),
        "col",
        split_axis=0,
        concat_axis=0,
        tiled=True,
    )
    pieces = pieces.reshape(row_devices, factor, slab_rows, tile_cols * channels)
    pieces = lax.all_to_all(pieces, "row", split_axis=0, concat_axis=2, tiled=True)
    pieces = pieces.reshape(factor, tile_cols, tile_cols, channels)
    return jnp.transpose(pieces, (0, 2, 1, 3)).reshape(factor * tile_cols, tile_cols, channels)


def on_device(pair_rep, ln_gain, ln_bias, w_in, w_out, w_pde, labels, pair_mask):
    tile_rows, tile_cols, channels = pair_rep.shape
    stride_rows = group_rows(tile_rows, tile_cols)
    blocks = pair_rep.reshape(tile_rows // stride_rows, stride_rows * tile_cols, channels)

    def forward(rows_block):
        return transition(rows_block, ln_gain, ln_bias, w_in, w_out)

    updated = lax.map(forward, blocks).reshape(tile_rows, tile_cols, channels)
    mask_float = pair_mask.astype(jnp.float32)
    local_count = jnp.sum(mask_float)
    valid_count = lax.psum(local_count, ("row", "col"))
    inverse_count = 1.0 / valid_count
    projected = jnp.einsum("ijc,cb->ijb", updated, w_pde, precision=lax.Precision.HIGHEST)
    scores = projected + mirror(projected)
    highest = jnp.max(scores, axis=-1, keepdims=True)
    shifted = jnp.exp(scores - highest)
    exp_total = jnp.sum(shifted, axis=-1, keepdims=True)
    log_total = highest + jnp.log(exp_total)
    bin_index = lax.broadcasted_iota(jnp.int32, (1, 1, scores.shape[2]), 2)
    onehot = (labels[:, :, None] == bin_index).astype(jnp.float32)
    picked = jnp.sum(scores * onehot, axis=-1, keepdims=True)
    local_loss = jnp.sum(mask_float * (log_total - picked)[:, :, 0])
    d_scores = mask_float[:, :, None] * (shifted / exp_total - onehot) * inverse_count
    d_sym = d_scores + mirror(d_scores)
    d_updated = jnp.einsum("ijb,cb->ijc", d_sym, w_pde, precision=lax.Precision.HIGHEST)
    grad_pde = jnp.einsum("ijc,ijb->cb", updated, d_sym, precision=lax.Precision.HIGHEST)
    cot_blocks = d_updated.reshape(blocks.shape)

    def backward(totals, pieces):
        rows_block, cotangent = pieces
        outcome, pullback = jax.vjp(transition, rows_block, ln_gain, ln_bias, w_in, w_out)
        gradients = pullback(cotangent)
        merged = tuple((earlier + later for earlier, later in zip(totals, gradients[1:])))
        return (merged, gradients[0])

    start_sums = (
        jnp.zeros_like(ln_gain),
        jnp.zeros_like(ln_bias),
        jnp.zeros_like(w_in),
        jnp.zeros_like(w_out),
    )
    param_sums, d_blocks = lax.scan(backward, start_sums, (blocks, cot_blocks))
    g_gain, g_bias, g_in, g_out = param_sums
    row_in, row_out = (
        lax.psum_scatter(g_in, "row", scatter_dimension=0, tiled=True),
        lax.psum_scatter(g_out, "row", scatter_dimension=0, tiled=True),
    )
    shard_in, shard_out = (
        lax.psum_scatter(row_in, "col", scatter_dimension=0, tiled=True),
        lax.psum_scatter(row_out, "col", scatter_dimension=0, tiled=True),
    )
    loss_sum, gain_sum, bias_sum, pde_sum = lax.psum(
        (local_loss, g_gain, g_bias, grad_pde), ("row", "col")
    )
    late_scale = 1.0
    mean_loss = loss_sum / valid_count
    d_pair_rep = d_blocks.reshape(pair_rep.shape) * late_scale
    return (
        mean_loss,
        d_pair_rep,
        gain_sum * late_scale,
        bias_sum * late_scale,
        shard_in * late_scale,
        shard_out * late_scale,
        pde_sum * late_scale,
    )


def solution(mesh):
    placed = (P("row", "col", None), P(), P(), P(), P(), P(), P("row", "col"), P("row", "col"))
    return jax.shard_map(
        on_device,
        mesh=mesh,
        in_specs=placed,
        out_specs=(
            P(),
            P("row", "col", None),
            P(),
            P(),
            P(("row", "col"), None),
            P(("row", "col"), None),
            P(),
        ),
        check_vma=False,
    )
```

profile of v0, /device:TPU:0, one launch (start us, length us, event | category | flops | bytes accessed | tf_op | source)
XLA Modules:
  0.0 227.3 jit_solution(3535305278162302303)
XLA Ops:
  7.2 0.0 copy-start
  7.2 0.0 copy-start.1
  7.2 1.0 reduce_sum.109
  8.2 0.1 div.52
  8.3 0.0 copy-done.1
  8.3 0.2 multiply_reduce_fusion.2
  8.5 0.1 add.95
  8.6 0.0 copy-start.3
  8.6 0.0 copy-start.6
  8.6 0.0 copy-done
  8.6 0.6 copy-done.3
  9.2 0.0 copy-done.6
  9.2 0.0 copy-start.7
  9.2 0.6 fusion.8
  9.9 0.3 copy-done.7
  10.2 0.0 copy-start.2
  10.2 0.4 fusion
  10.6 0.3 copy-done.2
  11.0 0.2 fusion.10
  11.2 0.1 reshape.118
  11.3 9.7 %all_to_all.76 = f32[2,4,2,512]{3,2,0,1:T(2,128)S(1)} all-to-all(f32[2,4,2,512]{3,2,0,1:T(2,128)S(1)} %copy.34), channel_id=1, replica_groups=mesh['row'=4,'col'=8] {'row'}, dimensions={1} | all-to-all | bytes 65536 | tf_op jit(solution)/shard_map/all_to_all | solution.py:48
  21.0 10.5 %all_to_all.77 = f32[8,1,2,512]{3,2,1,0:T(2,128)} all-to-all(f32[8,1,2,512]{3,2,1,0:T(2,128)S(1)} %bitcast.70), channel_id=1, replica_groups=mesh['row'=4,'col'=8] {'col'}, dimensions={0} | all-to-all | bytes 65536 | tf_op jit(solution)/shard_map/all_to_all | solution.py:47
  31.5 0.0 copy-start.4
  31.5 3.4 %all-to-all-start.2 = ((f32[4,2,2,512]{3,2,1,0:T(2,128)}), f32[4,2,2,512]{3,2,1,0:T(2,128)S(1)}, u32[]{:S(2)}, u32[]{:S(2)}) async-start(f32[4,2,2,512]{3,2,1,0:T(2,128)} %bitcast.7), calls=%async_computation.2 | async-start | bytes 65536 | tf_op jit(solution)/shard_map/all_to_all | solution.py:55
  34.9 0.0 copy-start.5
  34.9 0.0 reduce-scatter.9.cloned.1.call-start
  35.0 0.0 copy-done.4
  35.0 0.1 copy.38
  35.1 0.5 copy-done.5
  35.6 0.1 copy.33
  35.7 4.0 %all-to-all-done.2 = f32[4,2,2,512]{3,2,1,0:T(2,128)S(1)} async-done(((f32[4,2,2,512]{3,2,1,0:T(2,128)}), f32[4,2,2,512]{3,2,1,0:T(2,128)S(1)}, u32[]{:S(2)}, u32[]{:S(2)}) %all-to-all-start.2) | async-done | bytes 32800 | tf_op jit(solution)/shard_map/all_to_all | solution.py:55
  39.7 0.1 reshape.120
  39.8 0.1 fusion.26
  39.9 0.2 fusion.7
  40.1 0.6 convert_reduce_fusion
  40.7 38.5 %psum.36 = f32[]{:T(128)} all-reduce(f32[]{:T(128)} %get-tuple-element.57), channel_id=1, replica_groups=mesh['row'=4,'col'=8] {'row','col'}, use_global_device_ids=true, to_apply=%region_8.9 | all-reduce | flops 1 | bytes 8 | tf_op jit(solution)/shard_map/psum | solution.py:71
  79.9 0.1 multiply_multiply_fusion
  80.0 0.1 reshape.122
  80.1 8.4 %all_to_all.78 = f32[2,4,2,512]{3,2,0,1:T(2,128)S(1)} all-to-all(f32[2,4,2,512]{3,2,0,1:T(2,128)S(1)} %copy.39), channel_id=1, replica_groups=mesh['row'=4,'col'=8] {'row'}, dimensions={1} | all-to-all | bytes 65536 | tf_op jit(solution)/shard_map/all_to_all | solution.py:48
  88.5 8.4 %all_to_all.79 = f32[8,1,2,512]{3,2,1,0:T(2,128)S(1)} all-to-all(f32[8,1,2,512]{3,2,1,0:T(2,128)S(1)} %bitcast.71), channel_id=1, replica_groups=mesh['row'=4,'col'=8] {'col'}, dimensions={0} | all-to-all | bytes 65536 | tf_op jit(solution)/shard_map/all_to_all | solution.py:47
  96.9 7.1 %all_to_all.80 = f32[4,2,2,512]{3,2,1,0:T(2,128)S(1)} all-to-all(f32[4,2,2,512]{3,2,1,0:T(2,128)S(1)} %bitcast.72), channel_id=1, replica_groups=mesh['row'=4,'col'=8] {'row'}, dimensions={0} | all-to-all | bytes 65536 | tf_op jit(solution)/shard_map/all_to_all | solution.py:55
  104.0 0.1 reshape.124
  104.1 0.1 bitcast_add_fusion
  104.3 0.2 convolution_bitcast_fusion
  104.5 1.3 fusion.6
  105.8 0.0 reduce-scatter.9.cloned.1.call-update
  105.8 0.0 reduce-scatter.5.cloned.1.call-start
  105.9 0.4 fusion.23
  106.3 1.8 fusion.1
  108.1 0.0 reduce-scatter.5.cloned.1.call-update
  108.2 0.0 reduce-scatter.11.cloned.1.call-start
  108.2 0.7 multiply_reduce_fusion
  108.9 0.2 fusion.25
  109.2 17.6 %reduce-scatter.9.cloned.1.call-done = f32[128,128]{1,0:T(8,128)} async-done(((f32[512,128]{1,0:T(8,128)}), f32[128,128]{1,0:T(8,128)}) %reduce-scatter.9.cloned.1.call-update) | async-done | bytes 65552 | tf_op jit(solution)/shard_map/reduce_scatter | solution.py:106
  126.8 0.0 reduce-scatter.11.cloned.1.call-update
  126.8 0.0 reduce-scatter.7.cloned.1.call-start
  126.9 27.9 %reduce-scatter.5.cloned.1.call-done = f32[256,128]{1,0:T(8,128)} async-done(((f32[1024,128]{1,0:T(8,128)}), f32[256,128]{1,0:T(8,128)}) %reduce-scatter.5.cloned.1.call-update) | async-done | bytes 131088 | tf_op jit(solution)/shard_map/reduce_scatter | solution.py:105
  154.8 0.0 reduce-scatter.7.cloned.1.call-update
  154.8 0.3 convolution_bitcast_fusion.1
  155.1 40.2 %all-reduce.2 = (f32[]{:T(128)}, f32[128]{0:T(128)}, f32[128]{0:T(128)}, f32[128,64]{0,1:T(8,128)}) all-reduce(f32[]{:T(128)} %get-tuple-element.58, f32[128]{0:T(128)S(1)} %get-tuple-element.52, f32[128]{0:T(128)S(1)} %get-tuple-element.54, f32[128,64]{0,1:T(8,128)S(1)} %convolution_bitcast_fusion.1), channel_id=1, replica_groups=mesh['row'=4,'col'=8] {'row','col'}, use_global_device_ids=true, to_apply=%region_6.7 | all-reduce | flops 8449 | bytes 67592 | tf_op jit(solution)/shard_map/psum | solution.py:112
  196.6 0.7 add_bitcast_fusion
  197.4 0.0 reduce-scatter.11.cloned.1.call-done
  197.4 22.2 %reduce-scatter.7.cloned.1.call-done = f32[32,128]{1,0:T(8,128)} async-done(((f32[256,128]{1,0:T(8,128)}), f32[32,128]{1,0:T(8,128)}) %reduce-scatter.7.cloned.1.call-update) | async-done | bytes 16400 | tf_op jit(solution)/shard_map/reduce_scatter | solution.py:109
  (12 shorter events, 0.1 us)
Async XLA Ops:
  7.2 1.4 copy-start
  7.2 1.1 copy-start.1
  8.6 0.7 copy-start.3
  8.6 0.7 copy-start.6
  9.2 0.9 copy-start.7
  10.2 0.8 copy-start.2
  31.5 3.5 %copy-start.4 = (s32[16,8]{0,1:T(8,128)S(1)}, s32[16,8]{0,1:T(8,128)}, u32[]{:S(2)}) copy-start(s32[16,8]{0,1:T(8,128)} %param.14) | copy-start | bytes 1540
  31.5 8.1 %all-to-all-start.2 = ((f32[4,2,2,512]{3,2,1,0:T(2,128)}), f32[4,2,2,512]{3,2,1,0:T(2,128)S(1)}, u32[]{:S(2)}, u32[]{:S(2)}) async-start(f32[4,2,2,512]{3,2,1,0:T(2,128)} %bitcast.7), calls=%async_computation.2 | async-start | bytes 65536 | tf_op jit(solution)/shard_map/all_to_all | solution.py:55
  34.9 0.7 copy-start.5
  34.9 91.8 %reduce-scatter.9.cloned.1.call-start = ((), (), s32[]{:S(2)}) async-start(), calls=%async_computation.12 | async-start | bytes 327680 | tf_op jit(solution)/shard_map/reduce_scatter | solution.py:106
  105.8 49.0 %reduce-scatter.5.cloned.1.call-start = ((), (), s32[]{:S(2)}) async-start(), calls=%async_computation.10 | async-start | bytes 655360 | tf_op jit(solution)/shard_map/reduce_scatter | solution.py:105
  108.2 89.2 %reduce-scatter.11.cloned.1.call-start = ((), (), s32[]{:S(2)}) async-start(), calls=%async_computation.13 | async-start | bytes 73728 | tf_op jit(solution)/shard_map/reduce_scatter | solution.py:110
  126.8 92.8 %reduce-scatter.7.cloned.1.call-start = ((), (), s32[]{:S(2)}) async-start(), calls=%async_computation.11 | async-start | bytes 147456 | tf_op jit(solution)/shard_map/reduce_scatter | solution.py:109
Sparse Core Ops, SparseCore 0:
  105.9 20.8 reduce-scatter.8
  129.6 25.1 reduce-scatter.4
  157.6 30.5 reduce-scatter.10
  190.8 28.7 reduce-scatter.6
where the time goes:
time: 228 us; the launch traced here: 227 us
  blocking collectives  123 us (54%)
  waiting for transfers between devices  71.8 us (31%)
  between operations  17.2 us (8%)
  matrix products  6.04 us (3%)
  starting transfers between devices  3.56 us (2%)
  other arithmetic  3.27 us (1%)
  local copies, waits for them, and re-layouts  2.58 us (1%)
    psum x1, blocking collectives, on_device(): lax.psum((local_loss, g_gain, g_bias, grad_pde), ('row', 'col'))  40.2 us
    psum x1, blocking collectives, on_device(): valid_count = lax.psum(local_count, ('row', 'col'))  38.5 us
    reduce_scatter x1, waiting for transfers between devices, on_device(): lax.psum_scatter(g_in, 'row', scatter_dimension=0, tiled=True)  27.9 us
    reduce_scatter x1, waiting for transfers between devices, on_device(): lax.psum_scatter(row_in, 'col', scatter_dimension=0, tiled=True)  22.2 us
    all_to_all x2, blocking collectives, mirror(): lax.all_to_all(lax.all_to_all(pieces, 'row', split_axis=1, concat_axis=0,...  18.9 us
    all_to_all x2, blocking collectives, mirror(): lax.all_to_all(pieces, 'row', split_axis=1, concat_axis=0, tiled=True)  18.1 us
    reduce_scatter x1, waiting for transfers between devices, on_device(): lax.psum_scatter(g_out, 'row', scatter_dimension=0, tiled=True)  17.6 us
    all_to_all x1, blocking collectives, mirror(): lax.all_to_all(pieces, 'row', split_axis=0, concat_axis=2, tiled=True)  7.1 us
  transfers between devices with their start and end apart: 5, of which 4 were waited for; matrix products, arithmetic and copies ran while one was open for 2% of the time, Pallas kernels for 0%

commit v1 on v0

v1 whole, which is shorter than its diff:
```python
import functools

import jax
import jax.numpy as jnp
from jax import lax
from jax.experimental import pallas as pl
from jax.experimental.pallas import tpu as pltpu
from jax.sharding import PartitionSpec as P

epsilon = 1e-05
MESH = pl.DeviceIdType.MESH
HI = lax.Precision.HIGHEST


def mm(a, b, dims):
    return lax.dot_general(a, b, (dims, ((), ())), precision=HI, preferred_element_type=jnp.float32)


def dot_nn(a, b):
    return mm(a, b, ((1,), (0,)))


def dot_nt(a, b):
    return mm(a, b, ((1,), (1,)))


def dot_tn(a, b):
    return mm(a, b, ((0,), (0,)))


def remote(src, dst, sends, recvs, slot, device):
    return pltpu.make_async_remote_copy(
        src_ref=src,
        dst_ref=dst,
        send_sem=sends.at[slot],
        recv_sem=recvs.at[slot],
        device_id=device,
        device_id_type=MESH,
    )


def spread(values, tile_rows, tile_cols):
    pairs = tile_rows * tile_cols
    rows = jnp.broadcast_to(values[:, None, :], (tile_rows, tile_cols, tile_cols))
    rows = rows.reshape(pairs, tile_cols)
    place = lax.broadcasted_iota(jnp.int32, (pairs, tile_cols), 0) % tile_cols
    lane = lax.broadcasted_iota(jnp.int32, (pairs, tile_cols), 1)
    return jnp.sum(jnp.where(place == lane, rows, 0.0), axis=1, keepdims=True)


def kernel(
    sizes,
    x_ref, gain_ref, bias_ref, win_ref, wout_ref, wpde_ref, lab_ref, mask_ref,
    loss_out, dx_out, gain_out, bias_out, din_out, dout_out, pde_out,
    pair_send, pair_recv,
    small, small_core, small_row, small_z, small_last,
    norm, norm_core, norm_row, norm_z,
    go, go_core, go_row, go_sum, go_z,
    gi, gi_core, gi_row, gi_sum, gi_z,
    pair_ss, pair_rs, core_ss, core_rs, row_ss, row_rs, z_ss, z_rs, last_ss, last_rs,
):
    R, Z, tile_rows, tile_cols, bins, nb = sizes
    factor = tile_rows // tile_cols
    slab = tile_cols * tile_cols
    pairs = tile_rows * tile_cols
    r = lax.axis_index("row")
    c = lax.axis_index("col")
    core = c % 2
    z = c // 2
    sibling = z * 2 + 1 - core
    mirror_row = c // factor
    mirror_slab = c % factor
    channels = x_ref.shape[1]
    hidden_units = wout_ref.shape[0]

    barrier = pltpu.get_barrier_semaphore()

    def greet(row, col):
        pl.semaphore_signal(barrier, inc=1, device_id=(row, col), device_id_type=MESH)

    for k in range(factor):
        partner_col = r * factor + k

        @pl.when(jnp.logical_or(mirror_row != r, partner_col != c))
        def _():
            greet(mirror_row, partner_col)

    greet(r, sibling)
    for d in range(1, R):
        greet((r + d) % R, c)
        greet((r + d) % R, sibling)
    for e in range(1, Z):
        greet(r, ((z + e) % Z) * 2 + core)
    greeted = factor + 1 + 2 * (R - 1) + (Z - 1)

    x = x_ref[...]
    gain = gain_ref[...]
    average = jnp.mean(x, axis=-1, keepdims=True)
    centred = x - average
    variance = jnp.mean(centred * centred, axis=-1, keepdims=True)
    rstd = lax.rsqrt(variance + epsilon)
    xhat = centred * rstd
    normed = xhat * gain + bias_ref[...]
    gate = dot_nt(normed, win_ref[:hidden_units, :])
    up = dot_nt(normed, win_ref[hidden_units:, :])
    sig = 1.0 / (1.0 + jnp.exp(-gate))
    silu = gate * sig
    hidden = silu * up
    updated = x + dot_nn(hidden, wout_ref[...])
    w_pde = wpde_ref[...]
    projected = dot_nn(updated, w_pde)
    label = spread(lab_ref[...].astype(jnp.float32), tile_rows, tile_cols)
    mask = spread(mask_ref[...].astype(jnp.float32), tile_rows, tile_cols)
    bin_index = lax.broadcasted_iota(jnp.int32, (pairs, bins), 1).astype(jnp.float32)
    onehot = (bin_index == label).astype(jnp.float32)
    both = jnp.concatenate([projected, onehot], axis=1)
    pair_send[...] = both.reshape(factor, tile_cols, tile_cols, 2 * bins)

    @pl.when(mirror_row == r)
    def _():
        pl.semaphore_wait(barrier, greeted - 1)

    @pl.when(mirror_row != r)
    def _():
        pl.semaphore_wait(barrier, greeted)

    def pair_each(k, act, own):
        alone = jnp.logical_and(mirror_row == r, r * factor + k == c)

        @pl.when(jnp.logical_not(alone))
        def _():
            act(k)

        if own is not None:
            @pl.when(alone)
            def _():
                own(k)

    def start_pair(k):
        pltpu.make_async_remote_copy(
            src_ref=pair_send.at[k],
            dst_ref=pair_recv.at[mirror_slab],
            send_sem=pair_ss.at[k],
            recv_sem=pair_rs.at[mirror_slab],
            device_id=(mirror_row, r * factor + k),
            device_id_type=MESH,
        ).start()

    def own_pair(k):
        pair_recv[k] = pair_send[k]

    def wait_pair(k):
        taken = pltpu.make_async_remote_copy(
            src_ref=pair_send.at[k],
            dst_ref=pair_recv.at[k],
            send_sem=pair_ss.at[k],
            recv_sem=pair_rs.at[k],
            device_id=(mirror_row, r * factor + k),
            device_id_type=MESH,
        )
        taken.wait_recv()
        taken.wait_send()

    for k in range(factor):
        pair_each(k, start_pair, own_pair)
    for k in range(factor):
        pair_each(k, wait_pair, None)

    mirrored = jnp.concatenate(
        [
            jnp.concatenate([pair_recv[k, :, i, :] for i in range(tile_cols)], axis=0)
            for k in range(factor)
        ],
        axis=0,
    )
    total = both + mirrored
    scores = total[:, :bins]
    highest = jnp.max(scores, axis=-1, keepdims=True)
    shifted = jnp.exp(scores - highest)
    exp_total = jnp.sum(shifted, axis=-1, keepdims=True)
    log_total = highest + jnp.log(exp_total)
    picked = jnp.sum(scores * onehot, axis=-1, keepdims=True)
    loss = jnp.sum(mask * (log_total - picked))
    count = jnp.sum(mask)
    d_sym = mask * (2.0 * (shifted / exp_total) - total[:, bins:])

    def core_copy(wave, src, dst):
        return remote(src, dst, core_ss, core_rs, wave, (r, sibling))

    def row_copies(wave, src, dst):
        return [
            remote(src((r + d) % R), dst.at[r], row_ss, row_rs, wave * (R - 1) + d - 1, ((r + d) % R, c))
            for d in range(1, R)
        ]

    def z_copies(wave, src, dst):
        return [
            remote(
                src((z + e) % Z), dst.at[z], z_ss, z_rs, wave * (Z - 1) + e - 1, (r, ((z + e) % Z) * 2 + core)
            )
            for e in range(1, Z)
        ]

    def start(copies):
        for copy in copies:
            copy.start()

    def finish(copies):
        for copy in copies:
            copy.wait()

    def add_up(ref, count):
        value = ref[0]
        for s in range(1, count):
            value = value + ref[s]
        return value

    pde_t = dot_tn(d_sym, updated)
    top = small.shape[2] - 8
    row_index = lax.broadcasted_iota(jnp.int32, (8, channels), 0)
    meta = jnp.where(row_index == 0, loss, jnp.where(row_index == 1, count, 0.0))
    for a in range(2):
        for b in range(R):
            q = a * R + b
            small[a, b, :nb, :] = pde_t[q * nb:(q + 1) * nb, :]
            small[a, b, top:, :] = meta
    small_c = core_copy(0, small.at[1 - core], small_core)
    small_c.start()

    d_updated = dot_nt(d_sym, w_pde)
    go[...] = dot_tn(hidden, d_updated).reshape(go.shape)
    go_c = core_copy(1, go.at[:, :, 1 - core], go_core)
    go_c.start()

    d_hidden = dot_nt(d_updated, wout_ref[...])

    small_c.wait()
    small_core[...] = small_core[...] + small[core]
    small_row[r] = small_core[r]
    small_r = row_copies(0, lambda s: small_core.at[s], small_row)
    start(small_r)

    d_up = d_hidden * silu
    d_gate = d_hidden * up * (sig * (1.0 + gate * (1.0 - sig)))
    d_proj = jnp.concatenate([d_gate, d_up], axis=1)
    gi[...] = dot_tn(d_proj, normed).reshape(gi.shape)
    gi_c = core_copy(2, gi.at[:, :, 1 - core], gi_core)

    go_c.wait()
    gi_c.start()
    go_core[...] = go_core[...] + go[:, :, core]
    go_row[r] = go_core[r]
    go_r = row_copies(1, lambda s: go_core.at[s], go_row)
    start(go_r)

    d_normed = dot_nn(d_proj, win_ref[...])
    d_gain = jnp.sum(d_normed * xhat, axis=0, keepdims=True)
    d_bias = jnp.sum(d_normed, axis=0, keepdims=True)
    norm[...] = jnp.where(row_index == 0, d_gain, jnp.where(row_index == 1, d_bias, 0.0))
    norm_c = core_copy(3, norm, norm_core)
    norm_c.start()

    finish(small_r)
    small_z[z] = add_up(small_row, R)
    small_zc = z_copies(0, lambda s: small_z.at[z], small_z)
    start(small_zc)

    d_xhat = d_normed * gain
    first = jnp.mean(d_xhat, axis=-1, keepdims=True)
    second = jnp.mean(d_xhat * xhat, axis=-1, keepdims=True)
    dx = rstd * (d_xhat - first - xhat * second) + d_updated

    gi_c.wait()
    gi_core[...] = gi_core[...] + gi[:, :, core]
    gi_row[r] = gi_core[r]
    gi_r = row_copies(2, lambda s: gi_core.at[s], gi_row)
    start(gi_r)

    norm_c.wait()
    norm_core[...] = norm_core[...] + norm[...]
    norm_row[r] = norm_core[...]
    norm_r = row_copies(3, lambda s: norm_core, norm_row)
    start(norm_r)

    finish(go_r)
    go_sum[...] = add_up(go_row, R)
    go_zc = z_copies(1, lambda s: go_sum.at[s], go_z)
    start(go_zc)
    go_z[z] = go_sum[z]

    finish(small_zc)
    reduced = add_up(small_z, Z)
    whole_count = reduced[top + 1:top + 2, :]
    inverse = 1.0 / whole_count
    loss_out[...] = (reduced[top:top + 1, :] * inverse)[:, :1]
    mine = core * R + r
    small_last[mine] = reduced[:top]
    last = []
    for a in range(2):
        for d in range(R):
            if a or d:
                where = ((r + d) % R, z * 2 + (core + a) % 2)
                last.append(
                    remote(small_last.at[mine], small_last.at[mine], last_ss, last_rs, a * R + d - 1, where)
                )
    start(last)
    dx_out[...] = dx * inverse

    finish(gi_r)
    gi_sum[...] = add_up(gi_row, R)
    gi_zc = z_copies(2, lambda s: gi_sum.at[s], gi_z)
    start(gi_zc)
    gi_z[z] = gi_sum[z]
    finish(norm_r)
    norm_z[z] = add_up(norm_row, R)
    norm_zc = z_copies(3, lambda s: norm_z.at[z], norm_z)
    start(norm_zc)

    finish(go_zc)
    dout_out[...] = add_up(go_z, Z) * inverse
    finish(last)
    for q in range(2 * R):
        pde_out[q * nb:(q + 1) * nb, :] = small_last[q, :nb, :] * inverse
    finish(gi_zc)
    din_out[...] = add_up(gi_z, Z) * inverse
    finish(norm_zc)
    norm_all = add_up(norm_z, Z) * inverse
    gain_out[...] = norm_all[0:1]
    bias_out[...] = norm_all[1:2]


def on_device(pair_rep, ln_gain, ln_bias, w_in, w_out, w_pde, labels, pair_mask):
    tile_rows, tile_cols, channels = pair_rep.shape
    bins = w_pde.shape[1]
    R = lax.axis_size("row")
    Z = lax.axis_size("col") // 2
    owners = R * Z * 2
    pairs = tile_rows * tile_cols
    factor = tile_rows // tile_cols
    nb = bins // (2 * R)
    nbp = -(-nb // 8) * 8
    rows_i = w_in.shape[0] // owners
    rows_o = w_out.shape[0] // owners
    f32 = jnp.float32

    def vmem(*shape):
        return pltpu.VMEM(shape, f32)

    def wave(rows):
        return [
            vmem(R, Z, 2, rows, channels),
            vmem(R, Z, rows, channels),
            vmem(R, Z, rows, channels),
            vmem(Z, rows, channels),
            vmem(Z, rows, channels),
        ]

    dma = pltpu.SemaphoreType.DMA
    pair_send_shape = (factor, tile_cols, tile_cols, 2 * bins)
    scratch = [
        vmem(*pair_send_shape),
        vmem(*pair_send_shape),
        vmem(2, R, nbp + 8, channels),
        vmem(R, nbp + 8, channels),
        vmem(R, nbp + 8, channels),
        vmem(Z, nbp + 8, channels),
        vmem(2 * R, nbp, channels),
        vmem(8, channels),
        vmem(8, channels),
        vmem(R, 8, channels),
        vmem(Z, 8, channels),
        *wave(rows_o),
        *wave(rows_i),
        dma((factor,)),
        dma((factor,)),
        dma((4,)),
        dma((4,)),
        dma((4 * (R - 1),)),
        dma((4 * (R - 1),)),
        dma((4 * (Z - 1),)),
        dma((4 * (Z - 1),)),
        dma((2 * R - 1,)),
        dma((2 * R - 1,)),
    ]
    shape = jax.ShapeDtypeStruct
    loss, dx, gain, bias, d_in, d_out, pde_t = pl.pallas_call(
        functools.partial(kernel, (R, Z, tile_rows, tile_cols, bins, nb)),
        out_shape=[
            shape((1, 1), f32),
            shape((pairs, channels), f32),
            shape((1, channels), f32),
            shape((1, channels), f32),
            shape((rows_i, channels), f32),
            shape((rows_o, channels), f32),
            shape((bins, channels), f32),
        ],
        in_specs=[pl.BlockSpec(memory_space=pltpu.VMEM)] * 8,
        out_specs=[pl.BlockSpec(memory_space=pltpu.VMEM)] * 7,
        scratch_shapes=scratch,
        compiler_params=pltpu.CompilerParams(collective_id=0, has_side_effects=True),
        name="head_step",
    )(
        pair_rep.reshape(pairs, channels),
        ln_gain.reshape(1, channels),
        ln_bias.reshape(1, channels),
        w_in,
        w_out,
        w_pde,
        labels,
        pair_mask,
    )
    return (
        loss.reshape(()),
        dx.reshape(pair_rep.shape),
        gain.reshape(channels),
        bias.reshape(channels),
        d_in,
        d_out,
        pde_t.T,
    )


def solution(mesh):
    placed = (P("row", "col", None), P(), P(), P(), P(), P(), P("row", "col"), P("row", "col"))
    return jax.shard_map(
        on_device,
        mesh=mesh,
        in_specs=placed,
        out_specs=(
            P(),
            P("row", "col", None),
            P(),
            P(),
            P(("row", "col"), None),
            P(("row", "col"), None),
            P(),
        ),
        check_vma=False,
    )
```

time: 228 us -> 38.9 us (0.17)
  blocking collectives: 123 us -> 0 us
  waiting for transfers between devices: 71.8 us -> 0 us
  Pallas kernels: 0 us -> 28.3 us
  between operations: 17.2 us -> 2.44 us
  matrix products: 6.04 us -> 0 us
  local copies, waits for them, and re-layouts: 2.58 us -> 7.87 us
  starting transfers between devices: 3.56 us -> 0 us
  other arithmetic: 3.27 us -> 0 us
    psum x2 -> x0, blocking collectives: 78.7 us -> none  [the longest x1 40.2 us: on_device(): lax.psum((local_loss, g_gain, g_bias, grad_pde), ('row', 'col'))]
    reduce_scatter x4 -> x0, waiting for transfers between devices: 67.8 us -> none  [the longest x1 27.9 us: on_device(): lax.psum_scatter(g_in, 'row', scatter_dimension=0, tiled=True)]
    all_to_all x5 -> x0, blocking collectives: 44.1 us -> none  [the longest x2 18.9 us: mirror(): lax.all_to_all(lax.all_to_all(pieces, 'row', split_axis=1, concat_axis=0,...]
    pallas_call x0 -> x1, Pallas kernels: none -> 28.3 us  [on_device(): pl.pallas_call(functools.partial(kernel, (R, Z, tile_rows, tile_cols, bin...]
    dot_general x9 -> x0, matrix products: 6.04 us -> none  [the longest x3 3.18 us: transition(): lax.dot_general(normed, w_in, (((1,), (1,)), ((), ())), precision=lax.Pre...]
    unnamed x18 -> x23, local copies, waits for them, and re-layouts: 1.98 us -> 7.87 us
    all_to_all x1 -> x0, waiting for transfers between devices: 3.95 us -> none  [mirror(): lax.all_to_all(pieces, 'row', split_axis=0, concat_axis=2, tiled=True)]
    all_to_all x1 -> x0, starting transfers between devices: 3.39 us -> none  [mirror(): lax.all_to_all(pieces, 'row', split_axis=0, concat_axis=2, tiled=True)]
  transfers between devices with their start and end apart: 5 -> 0, of which waited for: 4 -> 0; matrix products, arithmetic and copies ran while one was open for 2% -> 0% of each run, Pallas kernels for 0% -> 0%
where the time goes in v1:
time: 38.9 us; the launch traced here: 38.6 us
  Pallas kernels  28.3 us (73%)
  local copies, waits for them, and re-layouts  7.87 us (20%)
  between operations  2.44 us (6%)
    pallas_call x1, Pallas kernels, on_device(): pl.pallas_call(functools.partial(kernel, (R, Z, tile_rows, tile_cols, bin...  28.3 us
    unnamed x23, local copies, waits for them, and re-layouts  7.87 us

profile of v1, /device:TPU:0, one launch (start us, length us, event | category | flops | bytes accessed | tf_op | source)
XLA Modules:
  0.0 38.6 jit_solution(9012074767704780729)
XLA Ops:
  0.6 0.0 copy-start.3
  0.6 0.7 %copy-done.3 = s32[16,8]{0,1:T(8,128)S(1)} copy-done((s32[16,8]{0,1:T(8,128)S(1)}, s32[16,8]{0,1:T(8,128)}, u32[]{:S(2)}) %copy-start.3) | copy-done | bytes 536
  1.3 0.0 copy-start.4
  1.3 0.7 %copy.16.lab_ref = s32[16,8]{1,0:T(8,128)} copy(s32[16,8]{0,1:T(8,128)S(1)} %copy-done.3) | data formatting | bytes 1024 | tf_op args[6]
  2.0 0.0 copy-done.4
  2.0 0.7 %copy.17.mask_ref = s32[16,8]{1,0:T(8,128)} copy(s32[16,8]{0,1:T(8,128)S(1)} %copy-done.4) | data formatting | bytes 1024 | tf_op args[7]
  2.7 1.5 %copy.15.wpde_ref = f32[128,64]{1,0:T(8,128)} copy(f32[128,64]{0,1:T(8,128)} %param.13) | data formatting | bytes 65536 | tf_op args[5]
  4.2 28.3 %head_step.1 = (f32[1,1]{1,0:T(1,128)}, f32[128,128]{1,0:T(8,128)}, f32[1,128]{1,0:T(1,128)}, f32[1,128]{1,0:T(1,128)}, f32[32,128]{1,0:T(8,128)}, /*index=5*/f32[16,128]{1,0:T(8,128)}, f32[64,128]{1,0:T(8,128)}) custom-call(f32[128,128]{1,0:T(8,128)} %bitcast.8, f32[1,128]{1,0:T(1,128)} %bitcast.11, f32[1,128]{1,0:T(1,128)} %bitcast.12, ...), custom_call_target="tpu_custom_call" | custom-call | tf_op jit(solution)/shard_map/head_step/pallas_call | solution.py:386
  33.1 0.0 copy-start.6
  33.1 0.0 copy-start.5
  33.1 0.0 copy-start.1
  33.1 0.0 copy-start.2
  33.1 1.5 %copy.26 = f32[16,8,128]{2,1,0:T(8,128)} copy(f32[16,8,128]{2,1,0:T(8,128)} %bitcast.9) | data formatting | bytes 131072
  34.6 0.0 copy-done.6
  34.6 0.0 copy-start
  34.6 0.5 %copy.27 = f32[128]{0:T(128)} copy(f32[128]{0:T(128)S(1)} %bitcast.14) | data formatting | bytes 1024
  35.1 0.0 copy-done.5
  35.1 0.5 %copy.28 = f32[128]{0:T(128)} copy(f32[128]{0:T(128)S(1)} %bitcast.13) | data formatting | bytes 1024
  35.6 0.0 copy-done.1
  35.6 0.6 %copy.29 = f32[32,128]{1,0:T(8,128)} copy(f32[32,128]{1,0:T(8,128)S(1)} %copy-done.1) | data formatting | bytes 32768
  36.2 0.0 copy-done.2
  36.2 0.6 %copy.30 = f32[16,128]{1,0:T(8,128)} copy(f32[16,128]{1,0:T(8,128)S(1)} %copy-done.2) | data formatting | bytes 16384
  36.8 0.0 copy-done
  36.8 0.6 %copy.31 = f32[128,64]{0,1:T(8,128)} copy(f32[128,64]{0,1:T(8,128)S(1)} %bitcast.10) | data formatting | bytes 65536
Async XLA Ops:
  0.6 0.7 %copy-start.3 = (s32[16,8]{0,1:T(8,128)S(1)}, s32[16,8]{0,1:T(8,128)}, u32[]{:S(2)}) copy-start(s32[16,8]{0,1:T(8,128)} %param.14) | copy-start | bytes 1540
  1.3 0.7 %copy-start.4 = (s32[16,8]{0,1:T(8,128)S(1)}, s32[16,8]{0,1:T(8,128)}, u32[]{:S(2)}) copy-start(s32[16,8]{0,1:T(8,128)} %param.15) | copy-start | bytes 1540
  33.1 1.5 %copy-start.6 = (f32[1,128]{1,0:T(1,128)S(1)}, f32[1,128]{1,0:T(1,128)}, u32[]{:S(2)}) copy-start(f32[1,128]{1,0:T(1,128)} %get-tuple-element.16) | copy-start | bytes 1540
  33.1 2.0 %copy-start.5 = (f32[1,128]{1,0:T(1,128)S(1)}, f32[1,128]{1,0:T(1,128)}, u32[]{:S(2)}) copy-start(f32[1,128]{1,0:T(1,128)} %get-tuple-element.17) | copy-start | bytes 1540
  33.1 2.5 %copy-start.1 = (f32[32,128]{1,0:T(8,128)S(1)}, f32[32,128]{1,0:T(8,128)}, u32[]{:S(2)}) copy-start(f32[32,128]{1,0:T(8,128)} %get-tuple-element.32) | copy-start | bytes 49156
  33.1 3.1 %copy-start.2 = (f32[16,128]{1,0:T(8,128)S(1)}, f32[16,128]{1,0:T(8,128)}, u32[]{:S(2)}) copy-start(f32[16,128]{1,0:T(8,128)} %get-tuple-element.33) | copy-start | bytes 24580
  34.6 2.2 %copy-start = (f32[64,128]{1,0:T(8,128)S(1)}, f32[64,128]{1,0:T(8,128)}, u32[]{:S(2)}) copy-start(f32[64,128]{1,0:T(8,128)} %get-tuple-element.20) | copy-start | bytes 98308

commit v2 on v1

--- a/solution.py
+++ b/solution.py
@@ -41,6 +41,7 @@
 
 def spread(values, tile_rows, tile_cols):
     pairs = tile_rows * tile_cols
+    values = values.T
     rows = jnp.broadcast_to(values[:, None, :], (tile_rows, tile_cols, tile_cols))
     rows = rows.reshape(pairs, tile_cols)
     place = lax.broadcasted_iota(jnp.int32, (pairs, tile_cols), 0) % tile_cols
@@ -108,7 +109,7 @@
     hidden = silu * up
     updated = x + dot_nn(hidden, wout_ref[...])
     w_pde = wpde_ref[...]
-    projected = dot_nn(updated, w_pde)
+    projected = dot_nt(updated, w_pde)
     label = spread(lab_ref[...].astype(jnp.float32), tile_rows, tile_cols)
     mask = spread(mask_ref[...].astype(jnp.float32), tile_rows, tile_cols)
     bin_index = lax.broadcasted_iota(jnp.int32, (pairs, bins), 1).astype(jnp.float32)
@@ -227,7 +228,7 @@
     small_c = core_copy(0, small.at[1 - core], small_core)
     small_c.start()
 
-    d_updated = dot_nt(d_sym, w_pde)
+    d_updated = dot_nn(d_sym, w_pde)
     go[...] = dot_tn(hidden, d_updated).reshape(go.shape)
     go_c = core_copy(1, go.at[:, :, 1 - core], go_core)
     go_c.start()
@@ -327,6 +328,18 @@
     norm_all = add_up(norm_z, Z) * inverse
     gain_out[...] = norm_all[0:1]
     bias_out[...] = norm_all[1:2]
+
+
+def put_out(*refs):
+    sems = refs[-1]
+    half = (len(refs) - 1) // 2
+    copies = [
+        pltpu.make_async_copy(refs[k], refs[half + k], sems.at[k]) for k in range(half)
+    ]
+    for copy in copies:
+        copy.start()
+    for copy in copies:
+        copy.wait()
 
 
 def on_device(pair_rep, ln_gain, ln_bias, w_in, w_out, w_pde, labels, pair_mask):
@@ -383,16 +396,16 @@
         dma((2 * R - 1,)),
     ]
     shape = jax.ShapeDtypeStruct
-    loss, dx, gain, bias, d_in, d_out, pde_t = pl.pallas_call(
+    held = pl.pallas_call(
         functools.partial(kernel, (R, Z, tile_rows, tile_cols, bins, nb)),
         out_shape=[
-            shape((1, 1), f32),
-            shape((pairs, channels), f32),
-            shape((1, channels), f32),
-            shape((1, channels), f32),
-            shape((rows_i, channels), f32),
-            shape((rows_o, channels), f32),
-            shape((bins, channels), f32),
+            vmem(1, 1),
+            vmem(pairs, channels),
+            vmem(1, channels),
+            vmem(1, channels),
+            vmem(rows_i, channels),
+            vmem(rows_o, channels),
+            vmem(bins, channels),
         ],
         in_specs=[pl.BlockSpec(memory_space=pltpu.VMEM)] * 8,
         out_specs=[pl.BlockSpec(memory_space=pltpu.VMEM)] * 7,
@@ -405,10 +418,19 @@
         ln_bias.reshape(1, channels),
         w_in,
         w_out,
-        w_pde,
-        labels,
-        pair_mask,
+        w_pde.T,
+        labels.T,
+        pair_mask.T,
     )
+    held = [pltpu.with_memory_space_constraint(value, pltpu.VMEM) for value in held]
+    loss, dx, gain, bias, d_in, d_out, pde_t = pl.pallas_call(
+        put_out,
+        out_shape=[shape(value.shape, f32) for value in held],
+        in_specs=[pl.BlockSpec(memory_space=pltpu.VMEM)] * 7,
+        out_specs=[pl.BlockSpec(memory_space=pl.ANY)] * 7,
+        scratch_shapes=[dma((7,))],
+        name="put_out",
+    )(*held)
     return (
         loss.reshape(()),
         dx.reshape(pair_rep.shape),

time: 38.9 us -> 30.4 us (0.78)
  local copies, waits for them, and re-layouts: 7.87 us -> 0 us
  between operations: 2.44 us -> 0.64 us
  Pallas kernels: 28.3 us -> 29.6 us
    unnamed x23 -> x0, local copies, waits for them, and re-layouts: 7.87 us -> none
    pallas_call x0 -> x1, Pallas kernels: none -> 1.35 us  [on_device(): pl.pallas_call(put_out, out_shape=[shape(value.shape, f32) for value in h...]
where the time goes in v2:
time: 30.4 us; the launch traced here: 30.2 us
  Pallas kernels  29.6 us (97%)
  between operations  0.64 us (2%)
    pallas_call x1, Pallas kernels, on_device(): pl.pallas_call(functools.partial(kernel, (R, Z, tile_rows, tile_cols, bin...  28.2 us
    pallas_call x1, Pallas kernels, on_device(): pl.pallas_call(put_out, out_shape=[shape(value.shape, f32) for value in h...  1.35 us

profile of v2, /device:TPU:0, one launch (start us, length us, event | category | flops | bytes accessed | tf_op | source)
XLA Modules:
  0.0 30.2 jit_solution(16676828277772415509)
XLA Ops:
  0.6 28.2 %head_step.1 = (f32[1,1]{1,0:T(1,128)}, f32[128,128]{1,0:T(8,128)S(1)}, f32[1,128]{1,0:T(1,128)S(1)}, f32[1,128]{1,0:T(1,128)S(1)}, f32[32,128]{1,0:T(8,128)S(1)...) custom-call(f32[128,128]{1,0:T(8,128)} %bitcast.11, f32[1,128]{1,0:T(1,128)} %bitcast.15, f32[1,128]{1,0:T(1,128)} %bitcast.16, ...), custom_call_target="tpu_custom_call" | custom-call | tf_op jit(solution)/shard_map/head_step/pallas_call | solution.py:399
  28.9 1.4 %put_out.1 = (f32[1,1]{1,0:T(1,128)}, f32[128,128]{1,0:T(8,128)}, f32[1,128]{1,0:T(1,128)}, f32[1,128]{1,0:T(1,128)}, f32[32,128]{1,0:T(8,128)}, /*index=5*/f32[16,128]{1,0:T(8,128)}, f32[64,128]{1,0:T(8,128)}) custom-call(f32[1,1]{1,0:T(1,128)} %get-tuple-element.21.refs_0_, f32[128,128]{1,0:T(8,128)S(1)} %get-tuple-element.22.refs_1_, ...), custom_call_target="tpu_custom_call" | custom-call | tf_op jit(solution)/shard_map/put_out/pallas_call | solution.py:426

commit v3 on v2

--- a/solution.py
+++ b/solution.py
@@ -51,13 +51,15 @@
 
 def kernel(
     sizes,
-    x_ref, gain_ref, bias_ref, win_ref, wout_ref, wpde_ref, lab_ref, mask_ref,
+    x_hbm, gain_hbm, bias_hbm, win_hbm, wout_hbm, wpde_hbm, lab_hbm, mask_hbm,
     loss_out, dx_out, gain_out, bias_out, din_out, dout_out, pde_out,
     pair_send, pair_recv,
     small, small_core, small_row, small_z, small_last,
     norm, norm_core, norm_row, norm_z,
     go, go_core, go_row, go_sum, go_z,
-    gi, gi_core, gi_row, gi_sum, gi_z,
+    ga, ga_core, ga_row, ga_sum, ga_z,
+    gb, gb_core, gb_row, gb_sum, gb_z,
+    x_ref, gain_ref, bias_ref, win_ref, wout_ref, wpde_ref, lab_ref, mask_ref, load_sems,
     pair_ss, pair_rs, core_ss, core_rs, row_ss, row_rs, z_ss, z_rs, last_ss, last_rs,
 ):
     R, Z, tile_rows, tile_cols, bins, nb = sizes
@@ -71,8 +73,8 @@
     sibling = z * 2 + 1 - core
     mirror_row = c // factor
     mirror_slab = c % factor
-    channels = x_ref.shape[1]
-    hidden_units = wout_ref.shape[0]
+    channels = x_hbm.shape[1]
+    hidden_units = wout_hbm.shape[0]
 
     barrier = pltpu.get_barrier_semaphore()
 
@@ -94,6 +96,20 @@
         greet(r, ((z + e) % Z) * 2 + core)
     greeted = factor + 1 + 2 * (R - 1) + (Z - 1)
 
+    loads = [
+        pltpu.make_async_copy(source, target, load_sems.at[k])
+        for k, (source, target) in enumerate(
+            (
+                (x_hbm, x_ref), (gain_hbm, gain_ref), (bias_hbm, bias_ref), (win_hbm, win_ref),
+                (wout_hbm, wout_ref), (wpde_hbm, wpde_ref), (lab_hbm, lab_ref), (mask_hbm, mask_ref),
+            )
+        )
+    ]
+    for load in loads:
+        load.start()
+
+    for load in loads[:3]:
+        load.wait()
     x = x_ref[...]
     gain = gain_ref[...]
     average = jnp.mean(x, axis=-1, keepdims=True)
@@ -102,12 +118,16 @@
     rstd = lax.rsqrt(variance + epsilon)
     xhat = centred * rstd
     normed = xhat * gain + bias_ref[...]
+    loads[3].wait()
     gate = dot_nt(normed, win_ref[:hidden_units, :])
     up = dot_nt(normed, win_ref[hidden_units:, :])
     sig = 1.0 / (1.0 + jnp.exp(-gate))
     silu = gate * sig
     hidden = silu * up
+    loads[4].wait()
     updated = x + dot_nn(hidden, wout_ref[...])
+    for load in loads[5:]:
+        load.wait()
     w_pde = wpde_ref[...]
     projected = dot_nt(updated, w_pde)
     label = spread(lab_ref[...].astype(jnp.float32), tile_rows, tile_cols)
@@ -234,7 +254,6 @@
     go_c.start()
 
     d_hidden = dot_nt(d_updated, wout_ref[...])
-
     small_c.wait()
     small_core[...] = small_core[...] + small[core]
     small_row[r] = small_core[r]
@@ -244,15 +263,32 @@
     d_up = d_hidden * silu
     d_gate = d_hidden * up * (sig * (1.0 + gate * (1.0 - sig)))
     d_proj = jnp.concatenate([d_gate, d_up], axis=1)
-    gi[...] = dot_tn(d_proj, normed).reshape(gi.shape)
-    gi_c = core_copy(2, gi.at[:, :, 1 - core], gi_core)
-
-    go_c.wait()
-    gi_c.start()
-    go_core[...] = go_core[...] + go[:, :, core]
-    go_row[r] = go_core[r]
-    go_r = row_copies(1, lambda s: go_core.at[s], go_row)
-    start(go_r)
+    half = ga.shape[3]
+    d_w_in = dot_tn(d_proj, normed).reshape(R, Z, 2, 2, half, channels)
+    ga[...] = d_w_in[:, :, :, 0]
+    gb[...] = d_w_in[:, :, :, 1]
+    ga_c = core_copy(2, ga.at[:, :, 1 - core], ga_core)
+    ga_c.start()
+    gb_c = core_copy(4, gb.at[:, :, 1 - core], gb_core)
+    gb_c.start()
+
+    def to_rows(wave, copy, own, got, across):
+        copy.wait()
+        got[...] = got[...] + own[:, :, core]
+        copies = row_copies(wave, lambda s: got.at[s], across)
+        start(copies)
+        across[r] = got[r]
+        return copies
+
+    def to_z(wave, copies, across, kept, along):
+        finish(copies)
+        kept[...] = add_up(across, R)
+        copies = z_copies(wave, lambda s: kept.at[s], along)
+        start(copies)
+        along[z] = kept[z]
+        return copies
+
+    go_r = to_rows(1, go_c, go, go_core, go_row)
 
     d_normed = dot_nn(d_proj, win_ref[...])
     d_gain = jnp.sum(d_normed * xhat, axis=0, keepdims=True)
@@ -261,21 +297,8 @@
     norm_c = core_copy(3, norm, norm_core)
     norm_c.start()
 
-    finish(small_r)
-    small_z[z] = add_up(small_row, R)
-    small_zc = z_copies(0, lambda s: small_z.at[z], small_z)
-    start(small_zc)
-
-    d_xhat = d_normed * gain
-    first = jnp.mean(d_xhat, axis=-1, keepdims=True)
-    second = jnp.mean(d_xhat * xhat, axis=-1, keepdims=True)
-    dx = rstd * (d_xhat - first - xhat * second) + d_updated
-
-    gi_c.wait()
-    gi_core[...] = gi_core[...] + gi[:, :, core]
-    gi_row[r] = gi_core[r]
-    gi_r = row_copies(2, lambda s: gi_core.at[s], gi_row)
-    start(gi_r)
+    ga_r = to_rows(2, ga_c, ga, ga_core, ga_row)
+    gb_r = to_rows(4, gb_c, gb, gb_core, gb_row)
 
     norm_c.wait()
     norm_core[...] = norm_core[...] + norm[...]
@@ -283,17 +306,20 @@
     norm_r = row_copies(3, lambda s: norm_core, norm_row)
     start(norm_r)
 
-    finish(go_r)
-    go_sum[...] = add_up(go_row, R)
-    go_zc = z_copies(1, lambda s: go_sum.at[s], go_z)
-    start(go_zc)
-    go_z[z] = go_sum[z]
-
+    d_xhat = d_normed * gain
+    first = jnp.mean(d_xhat, axis=-1, keepdims=True)
+    second = jnp.mean(d_xhat * xhat, axis=-1, keepdims=True)
+    dx = rstd * (d_xhat - first - xhat * second) + d_updated
+
+    finish(small_r)
+    small_z[z] = add_up(small_row, R)
+    small_zc = z_copies(0, lambda s: small_z.at[z], small_z)
+    start(small_zc)
+    go_zc = to_z(1, go_r, go_row, go_sum, go_z)
     finish(small_zc)
     reduced = add_up(small_z, Z)
     whole_count = reduced[top + 1:top + 2, :]
     inverse = 1.0 / whole_count
-    loss_out[...] = (reduced[top:top + 1, :] * inverse)[:, :1]
     mine = core * R + r
     small_last[mine] = reduced[:top]
     last = []
@@ -305,29 +331,31 @@
                     remote(small_last.at[mine], small_last.at[mine], last_ss, last_rs, a * R + d - 1, where)
                 )
     start(last)
+    loss_out[...] = (reduced[top:top + 1, :] * inverse)[:, :1]
     dx_out[...] = dx * inverse
 
-    finish(gi_r)
-    gi_sum[...] = add_up(gi_row, R)
-    gi_zc = z_copies(2, lambda s: gi_sum.at[s], gi_z)
-    start(gi_zc)
-    gi_z[z] = gi_sum[z]
+    ga_zc = to_z(2, ga_r, ga_row, ga_sum, ga_z)
+
     finish(norm_r)
     norm_z[z] = add_up(norm_row, R)
     norm_zc = z_copies(3, lambda s: norm_z.at[z], norm_z)
     start(norm_zc)
 
+    gb_zc = to_z(4, gb_r, gb_row, gb_sum, gb_z)
+
     finish(go_zc)
     dout_out[...] = add_up(go_z, Z) * inverse
-    finish(last)
-    for q in range(2 * R):
-        pde_out[q * nb:(q + 1) * nb, :] = small_last[q, :nb, :] * inverse
-    finish(gi_zc)
-    din_out[...] = add_up(gi_z, Z) * inverse
     finish(norm_zc)
     norm_all = add_up(norm_z, Z) * inverse
     gain_out[...] = norm_all[0:1]
     bias_out[...] = norm_all[1:2]
+    finish(ga_zc)
+    din_out[:half, :] = add_up(ga_z, Z) * inverse
+    finish(gb_zc)
+    din_out[half:, :] = add_up(gb_z, Z) * inverse
+    finish(last)
+    for q in range(2 * R):
+        pde_out[q * nb:(q + 1) * nb, :] = small_last[q, :nb, :] * inverse
 
 
 def put_out(*refs):
@@ -383,15 +411,25 @@
         vmem(R, 8, channels),
         vmem(Z, 8, channels),
         *wave(rows_o),
-        *wave(rows_i),
+        *wave(rows_i // 2),
+        *wave(rows_i // 2),
+        vmem(pairs, channels),
+        vmem(1, channels),
+        vmem(1, channels),
+        vmem(*w_in.shape),
+        vmem(*w_out.shape),
+        vmem(bins, channels),
+        pltpu.VMEM((tile_cols, tile_rows), labels.dtype),
+        pltpu.VMEM((tile_cols, tile_rows), pair_mask.dtype),
+        dma((8,)),
         dma((factor,)),
         dma((factor,)),
-        dma((4,)),
-        dma((4,)),
-        dma((4 * (R - 1),)),
-        dma((4 * (R - 1),)),
-        dma((4 * (Z - 1),)),
-        dma((4 * (Z - 1),)),
+        dma((5,)),
+        dma((5,)),
+        dma((5 * (R - 1),)),
+        dma((5 * (R - 1),)),
+        dma((5 * (Z - 1),)),
+        dma((5 * (Z - 1),)),
         dma((2 * R - 1,)),
         dma((2 * R - 1,)),
     ]
@@ -407,7 +445,7 @@
             vmem(rows_o, channels),
             vmem(bins, channels),
         ],
-        in_specs=[pl.BlockSpec(memory_space=pltpu.VMEM)] * 8,
+        in_specs=[pl.BlockSpec(memory_space=pl.ANY)] * 8,
         out_specs=[pl.BlockSpec(memory_space=pltpu.VMEM)] * 7,
         scratch_shapes=scratch,
         compiler_params=pltpu.CompilerParams(collective_id=0, has_side_effects=True),

time: 30.4 us -> 27.9 us (0.918)
  Pallas kernels: 29.6 us -> 27.1 us
    pallas_call x1, Pallas kernels: 28.2 us -> 25.7 us  [on_device(): pl.pallas_call(functools.partial(kernel, (R, Z, tile_rows, tile_cols, bin...]
where the time goes in v3:
time: 27.9 us; the launch traced here: 27.7 us
  Pallas kernels  27.1 us (97%)
  between operations  0.64 us (2%)
    pallas_call x1, Pallas kernels, on_device(): pl.pallas_call(functools.partial(kernel, (R, Z, tile_rows, tile_cols, bin...  25.7 us
    pallas_call x1, Pallas kernels, on_device(): pl.pallas_call(put_out, out_shape=[shape(value.shape, f32) for value in h...  1.35 us

profile of v3, /device:TPU:0, one launch (start us, length us, event | category | flops | bytes accessed | tf_op | source)
XLA Modules:
  0.0 27.7 jit_solution(10181926953318155361)
XLA Ops:
  0.6 25.7 %head_step.1 = (f32[1,1]{1,0:T(1,128)}, f32[128,128]{1,0:T(8,128)S(1)}, f32[1,128]{1,0:T(1,128)S(1)}, f32[1,128]{1,0:T(1,128)S(1)}, f32[32,128]{1,0:T(8,128)S(1)...) custom-call(f32[128,128]{1,0:T(8,128)} %bitcast.11, f32[1,128]{1,0:T(1,128)} %bitcast.15, f32[1,128]{1,0:T(1,128)} %bitcast.16, ...), custom_call_target="tpu_custom_call" | custom-call | tf_op jit(solution)/shard_map/head_step/pallas_call | solution.py:437
  26.4 1.4 %put_out.1 = (f32[1,1]{1,0:T(1,128)}, f32[128,128]{1,0:T(8,128)}, f32[1,128]{1,0:T(1,128)}, f32[1,128]{1,0:T(1,128)}, f32[32,128]{1,0:T(8,128)}, /*index=5*/f32[16,128]{1,0:T(8,128)}, f32[64,128]{1,0:T(8,128)}) custom-call(f32[1,1]{1,0:T(1,128)} %get-tuple-element.21.refs_0_, f32[128,128]{1,0:T(8,128)S(1)} %get-tuple-element.22.refs_1_, ...), custom_call_target="tpu_custom_call" | custom-call | tf_op jit(solution)/shard_map/put_out/pallas_call | solution.py:464

commit v4 on v3

--- a/solution.py
+++ b/solution.py
@@ -26,6 +26,21 @@
 
 def dot_tn(a, b):
     return mm(a, b, ((0,), (0,)))
+
+
+def two(value):
+    high = value.astype(jnp.bfloat16)
+    return high, (value - high.astype(jnp.float32)).astype(jnp.bfloat16)
+
+
+def mm3(a, b, dims):
+    a_high, a_low = two(a)
+    b_high, b_low = two(b)
+
+    def part(p, q):
+        return lax.dot_general(p, q, (dims, ((), ())), preferred_element_type=jnp.float32)
+
+    return part(a_high, b_high) + (part(a_high, b_low) + part(a_low, b_high))
 
 
 def remote(src, dst, sends, recvs, slot, device):
@@ -236,7 +251,23 @@
             value = value + ref[s]
         return value
 
-    pde_t = dot_tn(d_sym, updated)
+    def to_rows(wave, copy, own, got, across):
+        copy.wait()
+        got[...] = got[...] + own[:, :, core]
+        copies = row_copies(wave, lambda s: got.at[s], across)
+        start(copies)
+        across[r] = got[r]
+        return copies
+
+    def to_z(wave, copies, across, kept, along):
+        finish(copies)
+        kept[...] = add_up(across, R)
+        copies = z_copies(wave, lambda s: kept.at[s], along)
+        start(copies)
+        along[z] = kept[z]
+        return copies
+
+    pde_t = mm3(d_sym, updated, ((0,), (0,)))
     top = small.shape[2] - 8
     row_index = lax.broadcasted_iota(jnp.int32, (8, channels), 0)
     meta = jnp.where(row_index == 0, loss, jnp.where(row_index == 1, count, 0.0))
@@ -248,12 +279,12 @@
     small_c = core_copy(0, small.at[1 - core], small_core)
     small_c.start()
 
-    d_updated = dot_nn(d_sym, w_pde)
-    go[...] = dot_tn(hidden, d_updated).reshape(go.shape)
+    d_updated = mm3(d_sym, w_pde, ((1,), (0,)))
+    go[...] = mm3(hidden, d_updated, ((0,), (0,))).reshape(go.shape)
     go_c = core_copy(1, go.at[:, :, 1 - core], go_core)
     go_c.start()
 
-    d_hidden = dot_nt(d_updated, wout_ref[...])
+    d_hidden = mm3(d_updated, wout_ref[...], ((1,), (1,)))
     small_c.wait()
     small_core[...] = small_core[...] + small[core]
     small_row[r] = small_core[r]
@@ -263,8 +294,10 @@
     d_up = d_hidden * silu
     d_gate = d_hidden * up * (sig * (1.0 + gate * (1.0 - sig)))
     d_proj = jnp.concatenate([d_gate, d_up], axis=1)
+    go_r = to_rows(1, go_c, go, go_core, go_row)
+
     half = ga.shape[3]
-    d_w_in = dot_tn(d_proj, normed).reshape(R, Z, 2, 2, half, channels)
+    d_w_in = mm3(d_proj, normed, ((0,), (0,))).reshape(R, Z, 2, 2, half, channels)
     ga[...] = d_w_in[:, :, :, 0]
     gb[...] = d_w_in[:, :, :, 1]
     ga_c = core_copy(2, ga.at[:, :, 1 - core], ga_core)
@@ -272,25 +305,7 @@
     gb_c = core_copy(4, gb.at[:, :, 1 - core], gb_core)
     gb_c.start()
 
-    def to_rows(wave, copy, own, got, across):
-        copy.wait()
-        got[...] = got[...] + own[:, :, core]
-        copies = row_copies(wave, lambda s: got.at[s], across)
-        start(copies)
-        across[r] = got[r]
-        return copies
-
-    def to_z(wave, copies, across, kept, along):
-        finish(copies)
-        kept[...] = add_up(across, R)
-        copies = z_copies(wave, lambda s: kept.at[s], along)
-        start(copies)
-        along[z] = kept[z]
-        return copies
-
-    go_r = to_rows(1, go_c, go, go_core, go_row)
-
-    d_normed = dot_nn(d_proj, win_ref[...])
+    d_normed = mm3(d_proj, win_ref[...], ((1,), (0,)))
     d_gain = jnp.sum(d_normed * xhat, axis=0, keepdims=True)
     d_bias = jnp.sum(d_normed, axis=0, keepdims=True)
     norm[...] = jnp.where(row_index == 0, d_gain, jnp.where(row_index == 1, d_bias, 0.0))

time: 27.9 us -> 27.1 us (0.971)
  Pallas kernels: 27.1 us -> 26.3 us
    pallas_call x1, Pallas kernels: 25.7 us -> 25 us  [on_device(): pl.pallas_call(functools.partial(kernel, (R, Z, tile_rows, tile_cols, bin...]
where the time goes in v4:
time: 27.1 us; the launch traced here: 27 us
  Pallas kernels  26.3 us (97%)
  between operations  0.64 us (2%)
    pallas_call x1, Pallas kernels, on_device(): pl.pallas_call(functools.partial(kernel, (R, Z, tile_rows, tile_cols, bin...  25 us
    pallas_call x1, Pallas kernels, on_device(): pl.pallas_call(put_out, out_shape=[shape(value.shape, f32) for value in h...  1.35 us

profile of v4, /device:TPU:0, one launch (start us, length us, event | category | flops | bytes accessed | tf_op | source)
XLA Modules:
  0.0 27.0 jit_solution(1521030876805745783)
XLA Ops:
  0.6 25.0 %head_step.1 = (f32[1,1]{1,0:T(1,128)}, f32[128,128]{1,0:T(8,128)S(1)}, f32[1,128]{1,0:T(1,128)S(1)}, f32[1,128]{1,0:T(1,128)S(1)}, f32[32,128]{1,0:T(8,128)S(1)...) custom-call(f32[128,128]{1,0:T(8,128)} %bitcast.11, f32[1,128]{1,0:T(1,128)} %bitcast.15, f32[1,128]{1,0:T(1,128)} %bitcast.16, ...), custom_call_target="tpu_custom_call" | custom-call | tf_op jit(solution)/shard_map/head_step/pallas_call | solution.py:452
  25.6 1.4 %put_out.1 = (f32[1,1]{1,0:T(1,128)}, f32[128,128]{1,0:T(8,128)}, f32[1,128]{1,0:T(1,128)}, f32[1,128]{1,0:T(1,128)}, f32[32,128]{1,0:T(8,128)}, /*index=5*/f32[16,128]{1,0:T(8,128)}, f32[64,128]{1,0:T(8,128)}) custom-call(f32[1,1]{1,0:T(1,128)} %get-tuple-element.21.refs_0_, f32[128,128]{1,0:T(8,128)S(1)} %get-tuple-element.22.refs_1_, ...), custom_call_target="tpu_custom_call" | custom-call | tf_op jit(solution)/shard_map/put_out/pallas_call | solution.py:479

commit v5 on v4

--- a/solution.py
+++ b/solution.py
@@ -313,13 +313,13 @@
     norm_c.start()
 
     ga_r = to_rows(2, ga_c, ga, ga_core, ga_row)
-    gb_r = to_rows(4, gb_c, gb, gb_core, gb_row)
-
     norm_c.wait()
     norm_core[...] = norm_core[...] + norm[...]
     norm_row[r] = norm_core[...]
     norm_r = row_copies(3, lambda s: norm_core, norm_row)
     start(norm_r)
+
+    gb_r = to_rows(4, gb_c, gb, gb_core, gb_row)
 
     d_xhat = d_normed * gain
     first = jnp.mean(d_xhat, axis=-1, keepdims=True)

time: 27.1 us -> 26.9 us (level)
  no operation moved by 1% of the time
where the time goes in v5:
time: 26.9 us; the launch traced here: 26.8 us
  Pallas kernels  26.1 us (97%)
  between operations  0.64 us (2%)
    pallas_call x1, Pallas kernels, on_device(): pl.pallas_call(functools.partial(kernel, (R, Z, tile_rows, tile_cols, bin...  24.8 us
    pallas_call x1, Pallas kernels, on_device(): pl.pallas_call(put_out, out_shape=[shape(value.shape, f32) for value in h...  1.35 us

profile of v5, /device:TPU:0, one launch (start us, length us, event | category | flops | bytes accessed | tf_op | source)
XLA Modules:
  0.0 26.8 jit_solution(1083329054690252996)
XLA Ops:
  0.6 24.8 %head_step.1 = (f32[1,1]{1,0:T(1,128)}, f32[128,128]{1,0:T(8,128)S(1)}, f32[1,128]{1,0:T(1,128)S(1)}, f32[1,128]{1,0:T(1,128)S(1)}, f32[32,128]{1,0:T(8,128)S(1)...) custom-call(f32[128,128]{1,0:T(8,128)} %bitcast.11, f32[1,128]{1,0:T(1,128)} %bitcast.15, f32[1,128]{1,0:T(1,128)} %bitcast.16, ...), custom_call_target="tpu_custom_call" | custom-call | tf_op jit(solution)/shard_map/head_step/pallas_call | solution.py:452
  25.4 1.4 %put_out.1 = (f32[1,1]{1,0:T(1,128)}, f32[128,128]{1,0:T(8,128)}, f32[1,128]{1,0:T(1,128)}, f32[1,128]{1,0:T(1,128)}, f32[32,128]{1,0:T(8,128)}, /*index=5*/f32[16,128]{1,0:T(8,128)}, f32[64,128]{1,0:T(8,128)}) custom-call(f32[1,1]{1,0:T(1,128)} %get-tuple-element.21.refs_0_, f32[128,128]{1,0:T(8,128)S(1)} %get-tuple-element.22.refs_1_, ...), custom_call_target="tpu_custom_call" | custom-call | tf_op jit(solution)/shard_map/put_out/pallas_call | solution.py:479
